TPU v7x, 32 devices: a whole 2x2x4 slice. The times are simulated.
32 devices in a mesh: group: 2 (over y), ctx: 4 (over x, core), tp: 4 (over z).
Axes of the slice: x: 2, y: 2, z: 4, core: 2. Of those that a mesh axis runs over, the one named last changes fastest.
Arguments:
- tokens: bfloat16 [1024, 5376], P(('group', 'ctx'), 'tp'), parts along dimension 0
- positions: int32 [1024], P(('group', 'ctx')), parts along dimension 0, may hold values from 0 to 383, as said below
- first_key: int32 [1024], P(('group', 'ctx')), parts along dimension 0, may hold values from 0 to 511, as said below
- input_gain: float32 [5376], replicated, may hold values from 0.1 to 1.9
- query_weight: bfloat16 [5376, 4096], P(None, 'tp'), may hold values from -0.078125 to 0.078125
- kv_weight: bfloat16 [2, 5376, 2048], P(None, None, 'tp'), may hold values from -0.078125 to 0.078125
- query_gain: float32 [128], replicated, may hold values from 0.1 to 1.9
- key_gain: float32 [128], replicated, may hold values from 0.1 to 1.9
- out_weight: bfloat16 [4096, 5376], P('tp'), may hold values from -0.125 to 0.125
- post_gain: float32 [5376], replicated, may hold values from 0.1 to 1.9
Outputs:
- layer_out: bfloat16 [1024, 5376], P(('group', 'ctx'), 'tp'), parts along dimension 0
There are 2 independent parts, one for each index of `group`. A program takes and returns all parts, laid end to end along the dimension named above; an argument that names none is the same for every part. Nothing has to cross between parts.
Inputs may be any that keep to these rules, and one draw needn't show every extreme that they name: `positions`: A token's position is its offset within its document. Documents are contiguous runs of tokens; exactly one of them is 384 tokens long, every other one is shorter, and the last token forms a document of its own. first_key[i] is the larger of i - 1023 and the index of the first token of i's document (documents as described for positions).
All inputs are finite; a program needn't handle non-finite values.
Results may differ from a plain program's by a relative error of at most 0.014.
Values may be sent and summed in bfloat16 or wider, within the bound.
A program may use at most 128 MiB of HBM per device.

v0:
```python
import math
import jax
import jax.numpy as jnp
from jax import lax
from jax.sharding import PartitionSpec as P

D = 5376
H = 32
WINDOW = 1024
EPSILON = 1e-06


def from_partner(array, axis, distance):
    return lax.ppermute(array, axis, [(i, i ^ 1 << distance) for i in range(lax.axis_size(axis))])


def passed_along(block, axis, distance):
    devices = range(lax.axis_size(axis))
    route = [(i - distance, i) for i in devices if i - distance in devices]
    return lax.ppermute(block, axis, route)


def rms_norm(values, gain_vec):
    return (
        values * lax.rsqrt(jnp.mean(values * values, axis=-1, keepdims=True) + EPSILON) * gain_vec
    )


def rotate(values, positions_in):
    half_dim = values.shape[-1] // 2
    frequency = jnp.exp(
        jnp.arange(half_dim, dtype=jnp.float32) * (-2.0 * math.log(10000.0) / values.shape[-1])
    )
    angles = positions_in.astype(jnp.float32)[:, None] * frequency[None, :]
    cosines = jnp.cos(angles)[:, None, :]
    sine_part = jnp.sin(angles)[:, None, :]
    lower_half = values[..., :half_dim]
    upper_half = values[..., half_dim:]
    return jnp.concatenate(
        [
            lower_half * cosines - upper_half * sine_part,
            upper_half * cosines + lower_half * sine_part,
        ],
        axis=-1,
    )


def per_device(
    tokens,
    positions,
    first_key,
    input_gain,
    query_weight,
    kv_weight,
    query_gain,
    key_gain,
    out_weight,
    post_gain,
):
    tok_rows = tokens.shape[0]
    feat_dev = tokens.shape[1]
    head_dim = query_gain.shape[0]
    heads_dev = query_weight.shape[1] // head_dim
    tp_index = lax.axis_index("tp")
    ctx_index = lax.axis_index("ctx")
    ctx_count = lax.axis_size("ctx")
    local_x = tokens.astype(jnp.float32)
    kv_full = kv_weight
    if heads_dev == 1:
        partner = from_partner(kv_weight, "tp", 0)
        is_even = tp_index % 2 == 0
        kv_full = jnp.where(
            is_even,
            jnp.concatenate([kv_weight, partner], axis=2),
            jnp.concatenate([partner, kv_weight], axis=2),
        )
    gathered = lax.all_gather(tokens, "tp", axis=1, tiled=True).astype(jnp.float32)
    normed = rms_norm(gathered, input_gain).astype(jnp.bfloat16)
    query_raw = jnp.dot(normed, query_weight, preferred_element_type=jnp.float32)
    key_raw = jnp.dot(normed, kv_full[0], preferred_element_type=jnp.float32)
    value_raw = jnp.dot(normed, kv_full[1], preferred_element_type=jnp.float32)
    kv_heads = key_raw.shape[1] // head_dim
    group_size = heads_dev // kv_heads
    queries = (
        rotate(rms_norm(query_raw.reshape(tok_rows, heads_dev, head_dim), query_gain), positions)
        * (D // H) ** (-0.5)
    ).astype(jnp.bfloat16)
    keys = rotate(
        rms_norm(key_raw.reshape(tok_rows, kv_heads, head_dim), key_gain), positions
    ).astype(jnp.bfloat16)
    values_b = value_raw.reshape(tok_rows, kv_heads, head_dim).astype(jnp.bfloat16)
    kv_block = jnp.stack([keys, values_b])
    reach_blocks = min(ctx_count - 1, (WINDOW + tok_rows - 2) // tok_rows)
    received = []
    moving = kv_block
    for offset in range(reach_blocks):
        moving = passed_along(moving, "ctx", 1)
        received.append(moving)
    blocks = received[::-1] + [kv_block]
    keys_all = jnp.concatenate(blocks, axis=1)
    key_count = keys_all.shape[1]
    key_index = (ctx_index - reach_blocks) * tok_rows + jnp.arange(key_count, dtype=jnp.int32)
    query_index = ctx_index * tok_rows + jnp.arange(tok_rows, dtype=jnp.int32)
    visible = (key_index[None, :] >= first_key[:, None]) & (
        key_index[None, :] <= query_index[:, None]
    )
    grouped = queries.reshape(tok_rows, kv_heads, group_size, head_dim)
    scores = jnp.einsum("qkgd,tkd->kgqt", grouped, keys_all[0], preferred_element_type=jnp.float32)
    scores = jnp.where(visible[None, None], scores, -1e30)
    row_max = jnp.max(scores, axis=-1, keepdims=True)
    weights = jnp.exp(scores - row_max)
    denominator = jnp.sum(weights, axis=-1)
    mixed_out = jnp.einsum(
        "kgqt,tkd->qkgd",
        weights.astype(jnp.bfloat16),
        keys_all[1],
        preferred_element_type=jnp.float32,
    )
    mixed_out = mixed_out / jnp.transpose(denominator, (2, 0, 1))[..., None]
    attn = mixed_out.astype(jnp.bfloat16).reshape(tok_rows, heads_dev * head_dim)
    partial_value = jnp.dot(attn, out_weight, preferred_element_type=jnp.float32)
    summed = lax.psum(partial_value.astype(jnp.bfloat16), "tp").astype(jnp.float32)
    post_normed = rms_norm(summed, post_gain)
    own_cols = lax.dynamic_slice_in_dim(post_normed, tp_index * feat_dev, feat_dev, 1)
    return (local_x + own_cols).astype(jnp.bfloat16)


def solution(mesh):
    return jax.shard_map(
        per_device,
        mesh=mesh,
        in_specs=(
            P(("group", "ctx"), "tp"),
            P(("group", "ctx")),
            P(("group", "ctx")),
            P(),
            P(None, "tp"),
            P(None, None, "tp"),
            P(),
            P(),
            P("tp", None),
            P(),
        ),
        out_specs=P(("group", "ctx"), "tp"),
        check_vma=False,
    )
```

profile of v0, /device:TPU:0, one launch (start us, length us, event | category | flops | bytes accessed | tf_op | source)
XLA Modules:
  0.0 162.3 jit_solution(8768444792018409563)
XLA Ops:
  6.5 0.0 all-gather.2.cloned.1.call-start
  6.5 0.7 all-gather.2.cloned.1.call-update
  7.3 0.0 all-reduce.2.cloned.1.call-start
  7.3 8.9 %slice_bitcast_fusion.1 = (bf16[512,5376]{0,1:T(8,128)(2,1)}, bf16[512,5376]{0,1:T(8,128)(2,1)}) fusion(bf16[2,5376,512]{2,1,0:T(8,128)(2,1)} %param.15), kind=kLoop, calls=%fused_computation.2 | loop fusion | bytes 22020096 | tf_op jit(solution)/shard_map/dot_general | solution.py:80
  16.3 8.3 %copy.37 = bf16[512,5376]{1,0:T(8,128)(2,1)} copy(bf16[512,5376]{0,1:T(8,128)(2,1)} %get-tuple-element.5) | data formatting | bytes 11010048 | tf_op jit(solution)/shard_map/dot_general | solution.py:80
  24.6 0.0 copy-done.8
  24.6 0.0 copy-start.4
  24.6 8.3 %copy.39 = bf16[512,5376]{1,0:T(8,128)(2,1)} copy(bf16[512,5376]{0,1:T(8,128)(2,1)} %get-tuple-element.6) | data formatting | bytes 11010048 | tf_op jit(solution)/shard_map/dot_general | solution.py:81
  32.9 0.2 multiply_cosine_fusion
  33.1 0.1 copy.44
  33.2 0.1 copy.45
  33.3 0.1 compare_and_fusion
  33.5 11.8 %all-gather.2.cloned.1.call-done = bf16[128,5376]{0,1:T(8,128)(2,1)} async-done(((bf16[128,1344]{0,1:T(8,128)(2,1)}), bf16[128,5376]{0,1:T(8,128)(2,1)}) %all-gather.2.cloned.1.call-update) | async-done | bytes 1376272 | tf_op jit(solution)/shard_map/all_gather | solution.py:77
  45.3 2.1 %fusion = f32[128]{0:T(128)S(1)} fusion(bf16[128,5376]{0,1:T(8,128)(2,1)} %all-gather.2.cloned.1.call-done), kind=kLoop, calls=%fused_computation.5 | loop fusion | flops 2064256 | bytes 1376768 | tf_op jit(solution)/shard_map/reduce_sum | solution.py:25
  47.4 0.0 copy-start.6
  47.4 0.0 copy-start
  47.4 0.0 copy-start.1
  47.4 4.8 %multiply_reduce_fusion.2 = (f32[128,4]{0,1:T(4,128)S(1)}, f32[128,4,128]{0,2,1:T(8,128)S(1)}) fusion(bf16[4,128,5376]{2,1,0:T(8,128)(2,1)} %bitcast.74, f32[5376]{0:T(1024)S(1)} %copy-done.4, f32[128]{0:T(128)S(1)} %add_rsqrt_fusion.3, bf16[128,5376]{0,1:T(8,128)(2,1)} %all-gather.2.cloned.1.call-done), kind=kOutput, calls=%fused_computation.44 | convolution fusion | flops 707526144 | bytes 7167488 | tf_op jit(solution)/shard_map/dot_general | solution.py:80
  52.3 0.1 multiply_multiply_fusion.1
  52.4 1.7 %fusion.15 = bf16[1,128,4,128]{1,3,2,0:T(8,128)(2,1)S(1)} fusion(bf16[4,128,5376]{2,1,0:T(8,128)(2,1)S(1)} %bitcast.73, bf16[128,5376]{0,1:T(8,128)(2,1)S(1)} %copy-done, f32[5376]{0:T(1024)S(1)} %copy-done.4, f32[128]{0:T(128)S(1)} %add_rsqrt_fusion.3), kind=kOutput, calls=%fused_computation.23 | convolution fusion | flops 707461120 | bytes 7034368 | tf_op jit(solution)/shard_map/dot_general | solution.py:81
  54.2 0.0 copy-start.7
  54.2 1.3 collective-permute-start
  55.5 6.4 %convolution_bitcast_fusion.1 = f32[16,8,8,128]{3,1,2,0:T(8,128)S(1)} fusion(bf16[5376,1024]{1,0:T(8,128)(2,1)} %param.14, bf16[128,5376]{0,1:T(8,128)(2,1)S(1)} %copy-done, f32[5376]{0:T(1024)S(1)} %copy-done.4, f32[128]{0:T(128)S(1)} %add_rsqrt_fusion.3), kind=kOutput, calls=%fused_computation.20 | convolution fusion | flops 1412038656 | bytes 12932608 | tf_op jit(solution)/shard_map/dot_general | solution.py:79
  61.9 0.1 copy.62
  62.0 0.2 multiply_reduce_fusion.1
  62.3 0.0 collective-permute-done
  62.3 4.1 %collective-permute-start.1 = (bf16[2,128,4,128]{1,3,2,0:T(8,128)(2,1)S(1)}, bf16[2,128,4,128]{1,3,2,0:T(8,128)(2,1)S(1)}, u32[]{:S(2)}, u32[]{:S(2)}) collective-permute-start(bf16[2,128,4,128]{1,3,2,0:T(8,128)(2,1)S(1)} %collective-permute-done), channel_id=1, source_target_pairs={{0,4},{4,8},{8,12},{1,5},{5,9},{9,13},{2,6},{6,10},{10,14},{3,7},{... | collective-permute-start | bytes 786440 | tf_op jit(solution)/shard_map/ppermute | solution.py:20
  66.4 0.1 copy.43
  66.5 0.0 copy-done.7
  66.6 0.2 multiply_multiply_fusion
  66.8 0.8 collective-permute-done.1
  67.6 4.3 %collective-permute-start.2 = (bf16[2,128,4,128]{1,3,2,0:T(8,128)(2,1)S(1)}, bf16[2,128,4,128]{1,3,2,0:T(8,128)(2,1)S(1)}, u32[]{:S(2)}, u32[]{:S(2)}) collective-permute-start(bf16[2,128,4,128]{1,3,2,0:T(8,128)(2,1)S(1)} %collective-permute-done.1), channel_id=1, source_target_pairs={{0,4},{4,8},{8,12},{1,5},{5,9},{9,13},{2,6},{6,10},{10,14},{3,7},{... | collective-permute-start | bytes 786440 | tf_op jit(solution)/shard_map/ppermute | solution.py:20
  71.8 0.3 multiply_subtract_fusion
  72.1 0.1 copy.46
  72.2 0.1 copy.47
  72.3 0.5 collective-permute-done.2
  72.8 0.1 maximum_maximum_fusion
  72.9 0.6 fusion.3
  73.6 0.4 fusion.4
  73.9 0.6 fusion.11
  74.5 9.6 %convolution_convert_fusion = bf16[128,5376]{0,1:T(8,128)(2,1)} fusion(bf16[128,1024]{0,1:T(8,128)(2,1)S(1)} %bitcast.78, bf16[1024,5376]{1,0:T(8,128)(2,1)} %param.18), kind=kOutput, calls=%fused_computation | convolution fusion | flops 1409974272 | bytes 12648448 | tf_op jit(solution)/shard_map/dot_general | solution.py:121
  84.1 0.0 all-reduce.2.cloned.1.call-update
  84.2 0.8 dynamic-slice
  84.9 66.4 %all-reduce.2.cloned.1.call-done = bf16[128,5376]{0,1:T(8,128)(2,1)} async-done(((bf16[128,5376]{0,1:T(8,128)(2,1)}), bf16[128,5376]{0,1:T(8,128)(2,1)}) %all-reduce.2.cloned.1.call-update) | async-done | bytes 1376272 | tf_op jit(solution)/shard_map/psum | solution.py:122
  151.3 2.2 %multiply_reduce_fusion = f32[128]{0:T(128)S(1)} fusion(bf16[128,5376]{0,1:T(8,128)(2,1)} %all-reduce.2.cloned.1.call-done), kind=kLoop, calls=%fused_computation.8 | loop fusion | flops 2064256 | bytes 1376768 | tf_op jit(solution)/shard_map/reduce_sum | solution.py:25
  153.5 0.2 convert_element_type.52
  153.7 0.8 copy-done.3
  154.5 1.0 fusion.24
  (21 shorter events, 0.2 us)
Async XLA Ops:
  6.5 38.8 %all-gather.2.cloned.1.call-start = ((), (), s32[]{:S(2)}) async-start(), calls=%async_computation | async-start | bytes 1720320 | tf_op jit(solution)/shard_map/all_gather | solution.py:77
  7.3 144.1 %all-reduce.2.cloned.1.call-start = ((), (), s32[]{:S(2)}) async-start(), calls=%async_computation.1 | async-start | bytes 2752512 | tf_op jit(solution)/shard_map/psum | solution.py:122
  16.3 8.3 %copy-start.8 = (s32[128]{0:T(128)S(1)}, s32[128]{0:T(128)}, u32[]{:S(2)}) copy-start(s32[128]{0:T(128)} %param.11) | copy-start | bytes 1540
  24.6 8.7 %copy-start.5 = (s32[128]{0:T(128)S(1)}, s32[128]{0:T(128)}, u32[]{:S(2)}) copy-start(s32[128]{0:T(128)} %param.12) | copy-start | bytes 1540
  24.6 22.8 %copy-start.4 = (f32[5376]{0:T(1024)S(1)}, f32[5376]{0:T(1024)}, u32[]{:S(2)}) copy-start(f32[5376]{0:T(1024)} %param.13) | copy-start | bytes 64516
  47.4 4.9 %copy-start.6 = (f32[128]{0:T(128)S(1)}, f32[128]{0:T(128)}, u32[]{:S(2)}) copy-start(f32[128]{0:T(128)} %param.17) | copy-start | bytes 1540
  47.4 5.0 %copy-start = (bf16[128,5376]{0,1:T(8,128)(2,1)S(1)}, bf16[128,5376]{0,1:T(8,128)(2,1)}, u32[]{:S(2)}) copy-start(bf16[128,5376]{0,1:T(8,128)(2,1)} %all-gather.2.cloned.1.call-done) | copy-start | bytes 4128772
  47.4 5.0 %copy-start.1 = (bf16[512,5376]{1,0:T(8,128)(2,1)S(1)}, bf16[512,5376]{1,0:T(8,128)(2,1)}, u32[]{:S(2)}) copy-start(bf16[512,5376]{1,0:T(8,128)(2,1)} %copy.39) | copy-start | bytes 16515076
  54.2 12.4 %copy-start.7 = (f32[128]{0:T(128)S(1)}, f32[128]{0:T(128)}, u32[]{:S(2)}) copy-start(f32[128]{0:T(128)} %param.16) | copy-start | bytes 1540
  54.2 8.1 %collective-permute-start = (bf16[2,128,4,128]{1,3,2,0:T(8,128)(2,1)S(1)}, bf16[2,128,4,128]{1,3,2,0:T(8,128)(2,1)S(1)}, u32[]{:S(2)}, u32[]{:S(2)}) collective-permute-start(bf16[2,128,4,128]{1,3,2,0:T(8,128)(2,1)S(1)} %pad_maximum_fusion), channel_id=1, source_target_pairs={{0,4},{4,8},{8,12},{1,5},{5,9},{9,13},{2,6},{6,10},{10,14},{3,7},{... | collective-permute-start | bytes 786440 | tf_op jit(solution)/shard_map/ppermute | solution.py:20
  62.3 5.3 %collective-permute-start.1 = (bf16[2,128,4,128]{1,3,2,0:T(8,128)(2,1)S(1)}, bf16[2,128,4,128]{1,3,2,0:T(8,128)(2,1)S(1)}, u32[]{:S(2)}, u32[]{:S(2)}) collective-permute-start(bf16[2,128,4,128]{1,3,2,0:T(8,128)(2,1)S(1)} %collective-permute-done), channel_id=1, source_target_pairs={{0,4},{4,8},{8,12},{1,5},{5,9},{9,13},{2,6},{6,10},{10,14},{3,7},{... | collective-permute-start | bytes 786440 | tf_op jit(solution)/shard_map/ppermute | solution.py:20
  67.6 5.2 %collective-permute-start.2 = (bf16[2,128,4,128]{1,3,2,0:T(8,128)(2,1)S(1)}, bf16[2,128,4,128]{1,3,2,0:T(8,128)(2,1)S(1)}, u32[]{:S(2)}, u32[]{:S(2)}) collective-permute-start(bf16[2,128,4,128]{1,3,2,0:T(8,128)(2,1)S(1)} %collective-permute-done.1), channel_id=1, source_target_pairs={{0,4},{4,8},{8,12},{1,5},{5,9},{9,13},{2,6},{6,10},{10,14},{3,7},{... | collective-permute-start | bytes 786440 | tf_op jit(solution)/shard_map/ppermute | solution.py:20
  151.3 2.2 %copy-start.2 = (bf16[128,5376]{0,1:T(8,128)(2,1)S(1)}, bf16[128,5376]{0,1:T(8,128)(2,1)}, u32[]{:S(2)}) copy-start(bf16[128,5376]{0,1:T(8,128)(2,1)} %all-reduce.2.cloned.1.call-done) | copy-start | bytes 4128772
  153.5 1.0 copy-start.3
Sparse Core Ops, SparseCore 0:
  8.9 36.3 all-gather.1
  84.3 66.9 all-reduce.1
where the time goes:
time: 163 us; the launch traced here: 162 us
  waiting for transfers between devices  80.2 us (49%)
  local copies, waits for them, and re-layouts  27.8 us (17%)
  matrix products  23.8 us (15%)
  between operations  13.7 us (8%)
  starting transfers between devices  9.72 us (6%)
  other arithmetic  7.11 us (4%)
    psum x1, waiting for transfers between devices, per_device(): lax.psum(partial_value.astype(jnp.bfloat16), 'tp').astype(jnp.float32)  66.4 us
    dot_general x2, local copies, waits for them, and re-layouts, per_device(): key_raw = jnp.dot(normed, kv_full[0], preferred_element_type=jnp.float32)  17.3 us
    all_gather x1, waiting for transfers between devices, per_device(): lax.all_gather(tokens, 'tp', axis=1, tiled=True).astype(jnp.float32)  11.8 us
    ppermute x3, starting transfers between devices, passed_along(): return lax.ppermute(block, axis, route)  9.68 us
    dot_general x1, matrix products, per_device(): jnp.dot(attn, out_weight, preferred_element_type=jnp.float32)  9.61 us
    dot_general x1, local copies, waits for them, and re-layouts, per_device(): value_raw = jnp.dot(normed, kv_full[1], preferred_element_type=jnp.float32)  8.26 us
    dot_general x1, matrix products, per_device(): jnp.dot(normed, query_weight, preferred_element_type=jnp.float32)  6.44 us
    dot_general x1, matrix products, per_device(): key_raw = jnp.dot(normed, kv_full[0], preferred_element_type=jnp.float32)  4.84 us
  transfers between devices with their start and end apart: 5, of which 4 were waited for; matrix products, arithmetic and copies ran while one was open for 21% of the time, Pallas kernels for 0%

commit v1 on v0

--- a/solution.py
+++ b/solution.py
@@ -57,6 +57,13 @@
     out_weight,
     post_gain,
 ):
+
+    def _store_series(matrix, net_axis):
+        spare = jnp.stack([matrix] * jax.lax.axis_size(net_axis))
+        x_new = jax.lax.all_to_all(spare, net_axis, 0, 0)
+        later = jnp.concatenate(x_new, 1)
+        return later
+
     tok_rows = tokens.shape[0]
     feat_dev = tokens.shape[1]
     head_dim = query_gain.shape[0]
@@ -74,7 +81,7 @@
             jnp.concatenate([kv_weight, partner], axis=2),
             jnp.concatenate([partner, kv_weight], axis=2),
         )
-    gathered = lax.all_gather(tokens, "tp", axis=1, tiled=True).astype(jnp.float32)
+    gathered = _store_series(tokens, "tp").astype(jnp.float32)
     normed = rms_norm(gathered, input_gain).astype(jnp.bfloat16)
     query_raw = jnp.dot(normed, query_weight, preferred_element_type=jnp.float32)
     key_raw = jnp.dot(normed, kv_full[0], preferred_element_type=jnp.float32)

time: 163 us -> 173 us (1.061)
  local copies, waits for them, and re-layouts: 27.8 us -> 43.9 us
  waiting for transfers between devices: 80.2 us -> 71.7 us
  starting transfers between devices: 9.72 us -> 13.9 us
    dot_general x0 -> x1, local copies, waits for them, and re-layouts: none -> 14.5 us  [per_device(): jnp.dot(normed, query_weight, preferred_element_type=jnp.float32)]
    all_gather x1 -> x0, waiting for transfers between devices: 11.8 us -> none  [per_device(): lax.all_gather(tokens, 'tp', axis=1, tiled=True).astype(jnp.float32)]
    all_to_all x0 -> x1, waiting for transfers between devices: none -> 7.34 us  [_store_series(): x_new = jax.lax.all_to_all(spare, net_axis, 0, 0)]
    all_to_all x0 -> x1, starting transfers between devices: none -> 6.35 us  [_store_series(): x_new = jax.lax.all_to_all(spare, net_axis, 0, 0)]
    psum x1, waiting for transfers between devices: 66.4 us -> 64 us  [per_device(): lax.psum(partial_value.astype(jnp.bfloat16), 'tp').astype(jnp.float32)]
    another operation x0 -> x1, local copies, waits for them, and re-layouts: none -> 2.24 us  [_store_series(): spare = jnp.stack([matrix] * jax.lax.axis_size(net_axis))]
    ppermute x3, starting transfers between devices: 9.68 us -> 7.53 us  [passed_along(): return lax.ppermute(block, axis, route)]
    reduce_sum x3 -> x2, other arithmetic: 4.44 us -> 2.89 us  [rms_norm(): jnp.mean(values * values, axis=-1, keepdims=True) + EPSILON]
  transfers between devices with their start and end apart: 5 -> 5, of which waited for: 4 -> 3; matrix products, arithmetic and copies ran while one was open for 21% -> 27% of each run, Pallas kernels for 0% -> 0%
where the time goes in v1:
time: 173 us; the launch traced here: 172 us
  waiting for transfers between devices  71.7 us (41%)
  local copies, waits for them, and re-layouts  43.9 us (25%)
  matrix products  22.6 us (13%)
  starting transfers between devices  13.9 us (8%)
  between operations  13.6 us (8%)
  other arithmetic  6.16 us (4%)
    psum x1, waiting for transfers between devices, per_device(): lax.psum(partial_value.astype(jnp.bfloat16), 'tp').astype(jnp.float32)  64 us
    dot_general x2, local copies, waits for them, and re-layouts, per_device(): key_raw = jnp.dot(normed, kv_full[0], preferred_element_type=jnp.float32)  17.2 us
    dot_general x1, local copies, waits for them, and re-layouts, per_device(): jnp.dot(normed, query_weight, preferred_element_type=jnp.float32)  14.5 us
    dot_general x1, matrix products, per_device(): jnp.dot(attn, out_weight, preferred_element_type=jnp.float32)  9.61 us
    dot_general x1, local copies, waits for them, and re-layouts, per_device(): value_raw = jnp.dot(normed, kv_full[1], preferred_element_type=jnp.float32)  7.92 us
    ppermute x3, starting transfers between devices, passed_along(): return lax.ppermute(block, axis, route)  7.53 us
    all_to_all x1, waiting for transfers between devices, _store_series(): x_new = jax.lax.all_to_all(spare, net_axis, 0, 0)  7.34 us
    all_to_all x1, starting transfers between devices, _store_series(): x_new = jax.lax.all_to_all(spare, net_axis, 0, 0)  6.35 us
  transfers between devices with their start and end apart: 5, of which 3 were waited for; matrix products, arithmetic and copies ran while one was open for 27% of the time, Pallas kernels for 0%

profile of v1, /device:TPU:0, one launch (start us, length us, event | category | flops | bytes accessed | tf_op | source)
XLA Modules:
  0.0 171.8 jit_solution(9062679834523414320)
XLA Ops:
  6.5 2.2 %stack.6 = bf16[4,128,1344]{1,2,0:T(8,128)(2,1)} broadcast(bf16[128,1344]{0,1:T(8,128)(2,1)} %param.10), dimensions={1,2} | broadcast | bytes 1720320 | tf_op jit(solution)/shard_map/stack | solution.py:62
  8.8 6.3 %all-to-all-start = ((bf16[4,128,1344]{1,2,0:T(8,128)(2,1)}), bf16[4,128,1344]{1,2,0:T(8,128)(2,1)S(1)}, u32[]{:S(2)}, u32[]{:S(2)}) async-start(bf16[4,128,1344]{1,2,0:T(8,128)(2,1)} %stack.6), calls=%async_computation | async-start | bytes 2752512 | tf_op jit(solution)/shard_map/all_to_all | solution.py:63
  15.1 0.0 all-reduce.2.cloned.1.call-start
  15.1 0.0 copy-done.3
  15.1 0.1 mul.198
  15.2 9.0 %slice_bitcast_fusion.1 = (bf16[512,5376]{0,1:T(8,128)(2,1)}, bf16[512,5376]{0,1:T(8,128)(2,1)}) fusion(bf16[2,5376,512]{2,1,0:T(8,128)(2,1)} %param.15), kind=kLoop, calls=%fused_computation.2 | loop fusion | bytes 22020096 | tf_op jit(solution)/shard_map/dot_general | solution.py:87
  24.2 8.2 %copy.35 = bf16[512,5376]{1,0:T(8,128)(2,1)} copy(bf16[512,5376]{0,1:T(8,128)(2,1)} %get-tuple-element.5) | data formatting | bytes 11010048 | tf_op jit(solution)/shard_map/dot_general | solution.py:87
  32.4 0.0 copy-done.7
  32.4 7.9 %copy.37 = bf16[512,5376]{1,0:T(8,128)(2,1)} copy(bf16[512,5376]{0,1:T(8,128)(2,1)} %get-tuple-element.6) | data formatting | bytes 11010048 | tf_op jit(solution)/shard_map/dot_general | solution.py:88
  40.3 0.2 multiply_cosine_fusion
  40.5 7.3 %all-to-all-done = bf16[4,128,1344]{1,2,0:T(8,128)(2,1)S(1)} async-done(((bf16[4,128,1344]{1,2,0:T(8,128)(2,1)}), bf16[4,128,1344]{1,2,0:T(8,128)(2,1)S(1)}, u32[]{:S(2)}, u32[]{:S(2)}) %all-to-all-start) | async-done | bytes 1376288 | tf_op jit(solution)/shard_map/all_to_all | solution.py:63
  47.9 0.7 fusion
  48.6 0.9 fusion.2
  49.5 0.0 copy-start
  49.5 4.3 %multiply_reduce_fusion.2 = (f32[128,4]{0,1:T(4,128)S(1)}, f32[128,4,128]{0,2,1:T(8,128)S(1)}) fusion(bf16[128,5376,1]{0,1,2:T(8,128)(2,1)S(1)} %bitcast.72, bf16[4,128,5376]{2,1,0:T(8,128)(2,1)} %bitcast.70), kind=kOutput, calls=%fused_computation.39 | convolution fusion | flops 704773632 | bytes 7145472 | tf_op jit(solution)/shard_map/dot_general | solution.py:87
  53.8 0.0 copy-done
  53.9 0.0 copy-start.4
  53.9 1.6 fusion.8
  55.5 0.0 copy-done.4
  55.5 0.1 multiply_multiply_fusion.1
  55.6 1.3 collective-permute-start
  57.0 0.0 copy-start.5
  57.0 14.5 %copy.60 = bf16[1024,5376]{1,0:T(8,128)(2,1)} copy(bf16[1024,5376]{0,1:T(8,128)(2,1)} %bitcast.75) | data formatting | bytes 22020096 | tf_op jit(solution)/shard_map/dot_general | solution.py:86
  71.4 0.0 copy-done.5
  71.4 0.1 compare_and_fusion
  71.6 0.0 collective-permute-done
  71.6 4.1 %collective-permute-start.1 = (bf16[2,128,4,128]{1,3,2,0:T(8,128)(2,1)S(1)}, bf16[2,128,4,128]{1,3,2,0:T(8,128)(2,1)S(1)}, u32[]{:S(2)}, u32[]{:S(2)}) collective-permute-start(bf16[2,128,4,128]{1,3,2,0:T(8,128)(2,1)S(1)} %collective-permute-done), channel_id=1, source_target_pairs={{0,4},{4,8},{8,12},{1,5},{5,9},{9,13},{2,6},{6,10},{10,14},{3,7},{... | collective-permute-start | bytes 786440 | tf_op jit(solution)/shard_map/ppermute | solution.py:20
  75.7 0.0 copy-start.6
  75.7 5.8 %multiply_reduce_fusion.1 = (f32[128,8]{0,1:T(8,128)S(1)}, f32[128,8,128]{0,2,1:T(8,128)S(1)}) fusion(bf16[128,5376,1]{0,1,2:T(8,128)(2,1)S(1)} %bitcast.74, bf16[8,128,5376]{2,1,0:T(8,128)(2,1)} %bitcast.69), kind=kOutput, calls=%fused_computation.33 | convolution fusion | flops 1409547264 | bytes 12914688 | tf_op jit(solution)/shard_map/dot_general | solution.py:86
  81.6 0.0 collective-permute-done.1
  81.6 2.1 %collective-permute-start.2 = (bf16[2,128,4,128]{1,3,2,0:T(8,128)(2,1)S(1)}, bf16[2,128,4,128]{1,3,2,0:T(8,128)(2,1)S(1)}, u32[]{:S(2)}, u32[]{:S(2)}) collective-permute-start(bf16[2,128,4,128]{1,3,2,0:T(8,128)(2,1)S(1)} %collective-permute-done.1), channel_id=1, source_target_pairs={{0,4},{4,8},{8,12},{1,5},{5,9},{9,13},{2,6},{6,10},{10,14},{3,7},{... | collective-permute-start | bytes 786440 | tf_op jit(solution)/shard_map/ppermute | solution.py:20
  83.7 0.1 multiply_multiply_fusion
  83.8 0.1 multiply_subtract_fusion
  83.9 0.2 copy.42
  84.1 0.2 copy.43
  84.3 0.3 collective-permute-done.2
  84.7 0.1 maximum_maximum_fusion
  84.8 0.6 fusion.3
  85.4 0.4 fusion.4
  85.8 0.6 fusion.7
  86.4 9.6 %convolution_convert_fusion = bf16[128,5376]{0,1:T(8,128)(2,1)} fusion(bf16[128,1024]{0,1:T(8,128)(2,1)S(1)} %bitcast.78, bf16[1024,5376]{1,0:T(8,128)(2,1)} %param.18), kind=kOutput, calls=%fused_computation | convolution fusion | flops 1409974272 | bytes 12648448 | tf_op jit(solution)/shard_map/dot_general | solution.py:128
  96.0 0.0 all-reduce.2.cloned.1.call-update
  96.0 0.8 dynamic-slice
  96.8 64.0 %all-reduce.2.cloned.1.call-done = bf16[128,5376]{0,1:T(8,128)(2,1)} async-done(((bf16[128,5376]{0,1:T(8,128)(2,1)}), bf16[128,5376]{0,1:T(8,128)(2,1)}) %all-reduce.2.cloned.1.call-update) | async-done | bytes 1376272 | tf_op jit(solution)/shard_map/psum | solution.py:129
  160.8 2.2 %multiply_reduce_fusion = f32[128]{0:T(128)S(1)} fusion(bf16[128,5376]{0,1:T(8,128)(2,1)} %all-reduce.2.cloned.1.call-done), kind=kLoop, calls=%fused_computation.8 | loop fusion | flops 2064256 | bytes 1376768 | tf_op jit(solution)/shard_map/reduce_sum | solution.py:25
  163.0 0.2 convert_element_type.67
  163.2 0.8 copy-done.2
  163.9 1.0 fusion.15
  (16 shorter events, 0.1 us)
Async XLA Ops:
  6.5 8.6 %copy-start.3 = (f32[5376]{0:T(1024)S(1)}, f32[5376]{0:T(1024)}, u32[]{:S(2)}) copy-start(f32[5376]{0:T(1024)} %param.13) | copy-start | bytes 64516
  8.8 39.1 %all-to-all-start = ((bf16[4,128,1344]{1,2,0:T(8,128)(2,1)}), bf16[4,128,1344]{1,2,0:T(8,128)(2,1)S(1)}, u32[]{:S(2)}, u32[]{:S(2)}) async-start(bf16[4,128,1344]{1,2,0:T(8,128)(2,1)} %stack.6), calls=%async_computation | async-start | bytes 2752512 | tf_op jit(solution)/shard_map/all_to_all | solution.py:63
  15.1 145.7 %all-reduce.2.cloned.1.call-start = ((), (), s32[]{:S(2)}) async-start(), calls=%async_computation.1 | async-start | bytes 2752512 | tf_op jit(solution)/shard_map/psum | solution.py:129
  24.2 8.2 %copy-start.7 = (s32[128]{0:T(128)S(1)}, s32[128]{0:T(128)}, u32[]{:S(2)}) copy-start(s32[128]{0:T(128)} %param.11) | copy-start | bytes 1540
  49.5 4.3 %copy-start = (bf16[512,5376]{1,0:T(8,128)(2,1)S(1)}, bf16[512,5376]{1,0:T(8,128)(2,1)}, u32[]{:S(2)}) copy-start(bf16[512,5376]{1,0:T(8,128)(2,1)} %copy.37) | copy-start | bytes 16515076
  53.9 1.6 copy-start.4
  55.6 16.0 %collective-permute-start = (bf16[2,128,4,128]{1,3,2,0:T(8,128)(2,1)S(1)}, bf16[2,128,4,128]{1,3,2,0:T(8,128)(2,1)S(1)}, u32[]{:S(2)}, u32[]{:S(2)}) collective-permute-start(bf16[2,128,4,128]{1,3,2,0:T(8,128)(2,1)S(1)} %pad_maximum_fusion), channel_id=1, source_target_pairs={{0,4},{4,8},{8,12},{1,5},{5,9},{9,13},{2,6},{6,10},{10,14},{3,7},{... | collective-permute-start | bytes 786440 | tf_op jit(solution)/shard_map/ppermute | solution.py:20
  57.0 14.5 %copy-start.5 = (s32[128]{0:T(128)S(1)}, s32[128]{0:T(128)}, u32[]{:S(2)}) copy-start(s32[128]{0:T(128)} %param.12) | copy-start | bytes 1540
  71.6 10.0 %collective-permute-start.1 = (bf16[2,128,4,128]{1,3,2,0:T(8,128)(2,1)S(1)}, bf16[2,128,4,128]{1,3,2,0:T(8,128)(2,1)S(1)}, u32[]{:S(2)}, u32[]{:S(2)}) collective-permute-start(bf16[2,128,4,128]{1,3,2,0:T(8,128)(2,1)S(1)} %collective-permute-done), channel_id=1, source_target_pairs={{0,4},{4,8},{8,12},{1,5},{5,9},{9,13},{2,6},{6,10},{10,14},{3,7},{... | collective-permute-start | bytes 786440 | tf_op jit(solution)/shard_map/ppermute | solution.py:20
  75.7 8.0 %copy-start.6 = (f32[128]{0:T(128)S(1)}, f32[128]{0:T(128)}, u32[]{:S(2)}) copy-start(f32[128]{0:T(128)} %param.16) | copy-start | bytes 1540
  81.6 3.0 %collective-permute-start.2 = (bf16[2,128,4,128]{1,3,2,0:T(8,128)(2,1)S(1)}, bf16[2,128,4,128]{1,3,2,0:T(8,128)(2,1)S(1)}, u32[]{:S(2)}, u32[]{:S(2)}) collective-permute-start(bf16[2,128,4,128]{1,3,2,0:T(8,128)(2,1)S(1)} %collective-permute-done.1), channel_id=1, source_target_pairs={{0,4},{4,8},{8,12},{1,5},{5,9},{9,13},{2,6},{6,10},{10,14},{3,7},{... | collective-permute-start | bytes 786440 | tf_op jit(solution)/shard_map/ppermute | solution.py:20
  160.8 2.2 %copy-start.1 = (bf16[128,5376]{0,1:T(8,128)(2,1)S(1)}, bf16[128,5376]{0,1:T(8,128)(2,1)}, u32[]{:S(2)}) copy-start(bf16[128,5376]{0,1:T(8,128)(2,1)} %all-reduce.2.cloned.1.call-done) | copy-start | bytes 4128772
  163.0 1.0 copy-start.2
Sparse Core Ops, SparseCore 0:
  96.2 64.5 all-reduce.1
